TPU v7x, 32 devices: a whole 2x2x4 slice. The times are simulated.
32 devices in a mesh: grp: 2 (over x), bus: 16 (over z, y, core).
Axes of the slice: x: 2, y: 2, z: 4, core: 2. Of those that a mesh axis runs over, the one named last changes fastest.
Arguments:
- series: bfloat16 [32, 2048, 1024], P(('grp', 'bus')), parts along dimension 0, may hold values from -6 to 6
- hour_ids: int32 [32], P(('grp', 'bus')), parts along dimension 0, may hold values from 0 to 23
- hour_table: bfloat16 [24, 1024], replicated, may hold values from -3 to 3
- norm_gain: float32 [1024], replicated, may hold values from 0.1 to 1.9
- bus_order: int32 [4096], P('grp'), parts along dimension 0, may hold values from 0 to 2047, each once
- w_query: bfloat16 [1024, 512], replicated, may hold values from -0.1875 to 0.1875
- w_key: bfloat16 [1024, 512], replicated, may hold values from -0.1875 to 0.1875
- w_value: bfloat16 [1024, 512], replicated, may hold values from -0.1875 to 0.1875
- score_scale: float32 [8], replicated, may hold values from 0.5 to 10, as said below
- neighbors: int32 [32, 3], P('grp'), parts along dimension 0, may hold values from -1 to 15, as said below
- grad_out: bfloat16 [32, 2048, 512], P('grp', 'bus'), parts along dimension 0, may hold values from -6 to 6
Outputs:
- key_grad: bfloat16 [32, 2048, 512], P('grp', 'bus'), parts along dimension 0
- value_grad: bfloat16 [32, 2048, 512], P('grp', 'bus'), parts along dimension 0
There are 2 independent parts, one for each index of `grp`. A program takes and returns all parts, laid end to end along the dimension named above; an argument that names none is the same for every part. Nothing has to cross between parts.
Inputs may be any that keep to these rules, and one draw needn't show every extreme that they name: `neighbors`: row b lists the key blocks read by query block b: entry 0 is b - 1 or -1, entry 1 is b, entry 2 is b + 1 or -1; -1 marks a block not read, and stands in entry 0 of row 0 and entry 2 of row 15. `score_scale`: positive temperatures of the heads.
All inputs are finite; a program needn't handle non-finite values.
Results may differ from a plain program's by a relative error of at most 0.018.
The roundings to bfloat16 on the way count: a program that leaves them out, or rounds other values in their place, can miss the bound.
Values may be sent and summed in bfloat16 or wider, within the bound.
No kernel may reach another device: no remote copies, remote signals or barrier semaphores. Data moves between devices by JAX's collectives and lax.ppermute only.
A program may use at most 256 MiB of HBM per device.

v0:
```python
import math
import jax
import jax.numpy as jnp
from jax import lax
from jax.sharding import PartitionSpec as P

EPSILON = 1e-05
NEG_FILL = -1e30


def with_halo(shard, sides, width):
    for axis, dim in sides:
        devices, length = (lax.axis_size(axis), shard.shape[dim])
        up = [(i, (i + 1) % devices) for i in range(devices - 1)]
        down = [(j, i) for i, j in up]
        last = lax.slice_in_dim(shard, length - width, length, axis=dim)
        leading = lax.slice_in_dim(shard, 0, width, axis=dim)
        before = lax.ppermute(last, axis, up)
        after = lax.ppermute(leading, axis, down)
        shard = jnp.concatenate([before, shard, after], axis=dim)
    return shard


def from_behind(value, axis, steps):
    count = lax.axis_size(axis)
    leading, last = (max(0, -steps), min(count, count - steps))
    return lax.ppermute(value, axis, [(source, source + steps) for source in range(leading, last)])


def split_heads(array, head_count):
    return array.reshape(array.shape[0], array.shape[1], head_count, array.shape[2] // head_count)


def over_groups(step_fn, arrays, group_size):
    stacked = tuple(
        (
            item.reshape((item.shape[0] // group_size, group_size) + item.shape[1:])
            for item in arrays
        )
    )
    results = lax.map(lambda pieces: step_fn(*pieces), stacked)
    return tuple((item.reshape((-1,) + item.shape[2:]) for item in results))


def reader_terms(queries, key_tiles, value_tiles, grad_rows, colvalid, head_scale):
    scores = (
        jnp.einsum("sihd,sjhd->shij", queries, key_tiles, preferred_element_type=jnp.float32)
        * head_scale[None, :, None, None]
    )
    scores = jnp.where(colvalid[None, None, None, :], scores, NEG_FILL)
    row_max = jnp.max(scores, axis=-1)
    log_total = row_max + jnp.log(jnp.sum(jnp.exp(scores - row_max[..., None]), axis=-1))
    weights = jnp.exp(scores - log_total[..., None])
    weights_b = weights.astype(jnp.bfloat16)
    attended = jnp.einsum(
        "shij,sjhd->sihd", weights_b, value_tiles, preferred_element_type=jnp.float32
    ).astype(jnp.bfloat16)
    row_dot = jnp.einsum("sihd,sihd->shi", grad_rows, attended, preferred_element_type=jnp.float32)
    dweights = jnp.einsum(
        "sihd,sjhd->shij", grad_rows, value_tiles, preferred_element_type=jnp.float32
    )
    dscores = (weights * (dweights - row_dot[..., None]) * head_scale[None, :, None, None]).astype(
        jnp.bfloat16
    )
    value_part = jnp.einsum(
        "shij,sihd->sjhd", weights_b, grad_rows, preferred_element_type=jnp.float32
    )
    key_part = jnp.einsum("shij,sihd->sjhd", dscores, queries, preferred_element_type=jnp.float32)
    return (log_total, row_dot, key_part.astype(jnp.bfloat16), value_part.astype(jnp.bfloat16))


def on_device(
    series,
    hour_ids,
    hour_table,
    norm_gain,
    bus_order,
    w_query,
    w_key,
    w_value,
    score_scale,
    neighbors,
    grad_out,
):
    head_count = score_scale.shape[0]
    snap_count = grad_out.shape[0]
    block_rows = grad_out.shape[1]
    feat_width = grad_out.shape[2]
    head_dim = feat_width // head_count
    ordered = jnp.take(series, bus_order, axis=1)
    onehot = (
        hour_ids[:, None] == jnp.arange(hour_table.shape[0], dtype=jnp.int32)[None, :]
    ).astype(jnp.bfloat16)
    hour_rows = jnp.dot(onehot, hour_table, preferred_element_type=jnp.float32)
    mixed = ordered.astype(jnp.float32) + hour_rows[:, None, :]
    normed = (
        mixed * lax.rsqrt(jnp.mean(mixed * mixed, axis=-1, keepdims=True) + EPSILON) * norm_gain
    ).astype(jnp.bfloat16)
    arrived = lax.all_to_all(normed, "bus", split_axis=1, concat_axis=0, tiled=True)
    flat_rows = arrived.reshape(-1, arrived.shape[2])
    queries, key_rows, value_rows = [
        jnp.dot(flat_rows, weight, preferred_element_type=jnp.float32)
        .astype(jnp.bfloat16)
        .reshape(snap_count, block_rows, feat_width)
        for weight in (w_query, w_key, w_value)
    ]
    dev_index = lax.axis_index("bus")
    own_row = lax.dynamic_slice_in_dim(neighbors, dev_index, 1, 0)[0]
    colvalid = jnp.repeat(own_row >= 0, block_rows)
    head_scale = score_scale / math.sqrt(head_dim)
    group_size = math.gcd(snap_count, max(1, 512 // block_rows))
    kv_tiles = with_halo(jnp.stack([key_rows, value_rows]), (("bus", 2),), block_rows)
    query_heads = split_heads(queries, head_count)
    grad_heads = split_heads(grad_out, head_count)
    key_heads = split_heads(kv_tiles[0], head_count)
    value_heads = split_heads(kv_tiles[1], head_count)

    def full_step(query_part, key_part, value_part, grad_part):
        return reader_terms(query_part, key_part, value_part, grad_part, colvalid, head_scale)

    log_total, row_dot, key_part, value_part = over_groups(
        full_step, (query_heads, key_heads, value_heads, grad_heads), group_size
    )
    partials = jnp.stack(
        [
            key_part.reshape(snap_count, 3 * block_rows, feat_width),
            value_part.reshape(snap_count, 3 * block_rows, feat_width),
        ]
    )
    from_upper = from_behind(partials[:, :, :block_rows], "bus", -1)
    from_lower = from_behind(partials[:, :, 2 * block_rows :], "bus", 1)
    summed = (
        partials[:, :, block_rows : 2 * block_rows].astype(jnp.float32)
        + from_lower.astype(jnp.float32)
        + from_upper.astype(jnp.float32)
    )
    key_grad = summed[0].astype(jnp.bfloat16)
    value_grad = summed[1].astype(jnp.bfloat16)
    return (key_grad, value_grad)


def solution(mesh):
    return jax.shard_map(
        on_device,
        mesh=mesh,
        in_specs=(
            P(("grp", "bus"), None, None),
            P(("grp", "bus")),
            P(),
            P(),
            P("grp"),
            P(),
            P(),
            P(),
            P(),
            P("grp", None),
            P("grp", "bus", None),
        ),
        out_specs=(P("grp", "bus", None), P("grp", "bus", None)),
        check_vma=False,
    )
```

profile of v0, /device:TPU:12, one launch (start us, length us, event | category | flops | bytes accessed | tf_op | source)
XLA Modules:
  0.0 511.9 jit_solution(18104541909109588138)
XLA Ops:
  2.8 13.7 %gather_fusion = bf16[2048,1024]{1,0:T(8,128)(2,1)} fusion(bf16[2048,1024]{1,0:T(8,128)(2,1)} %bitcast.128, s32[2048]{0:T(1024)S(1)} %fusion.71), kind=kCustom, calls=%fused_computation | custom fusion | bytes 8396800 | tf_op jit(solution)/shard_map/jit(_take)/gather | solution.py:90
  16.6 3.6 multiply_reduce_fusion
  22.0 28.7 %copy.65 = bf16[1,2048,1024]{2,0,1:T(2,128)(2,1)} copy(bf16[1,2048,1024]{2,1,0:T(8,128)(2,1)S(1)} %multiply_convert_fusion.6) | data formatting | bytes 8388608 | tf_op jit(solution)/shard_map/convert_element_type | solution.py:98
  51.3 25.9 %reduce.5 = bf16[2048,1024]{1,0:T(8,128)(2,1)} reduce(bf16[2048,1,1024]{2,1,0:T(2,128)(2,1)} %bitcast.129, bf16[]{:T(256)} %broadcast.169), dimensions={1}, to_apply=%bitcast.102.reduce_sub_computation | reduce | bytes 8388610
  77.2 11.4 %reshape.223 = bf16[16,2,65536]{2,1,0:T(2,128)(2,1)} reshape(bf16[2048,1024]{1,0:T(8,128)(2,1)} %reduce.5) | data formatting | bytes 8388608
  88.6 98.4 %all_to_all.4 = bf16[16,2,65536]{2,1,0:T(2,128)(2,1)} all-to-all(bf16[16,2,65536]{2,1,0:T(2,128)(2,1)} %reshape.223), channel_id=1, replica_groups=mesh['grp'=2,'bus'=16] {'bus'}, dimensions={0} | all-to-all | bytes 8388608 | tf_op jit(solution)/shard_map/all_to_all | solution.py:99
  187.0 12.3 %reshape.224 = bf16[2048,1,1024]{2,1,0:T(2,128)(2,1)} reshape(bf16[16,2,65536]{2,1,0:T(2,128)(2,1)} %all_to_all.4) | data formatting | bytes 8388608
  199.3 7.1 %fusion.65 = bf16[2048,512]{1,0:T(8,128)(2,1)} fusion(bf16[1024,512]{1,0:T(8,128)(2,1)S(1)} %copy-done, bf16[1,2048,1024]{2,0,1:T(2,128)(2,1)} %bitcast.135), kind=kOutput, calls=%fused_computation.64 | convolution fusion | flops 2148532224 | bytes 7340032 | tf_op jit(solution)/shard_map/dot_general | solution.py:102
  206.4 3.0 copy.36
  209.5 7.3 %fusion.68 = bf16[2048,512]{1,0:T(8,128)(2,1)} fusion(bf16[1024,512]{1,0:T(8,128)(2,1)} %param.20, bf16[1,2048,1024]{2,0,1:T(2,128)(2,1)} %bitcast.136), kind=kOutput, calls=%fused_computation.65 | convolution fusion | flops 2148532224 | bytes 7340032 | tf_op jit(solution)/shard_map/dot_general | solution.py:102
  216.8 3.9 copy.37
  220.7 3.9 pad_maximum_fusion.2
  224.7 2.2 collective-permute-start
  226.9 3.6 collective-permute-start.1
  230.5 3.9 copy.38
  234.6 7.3 %fusion.62 = bf16[2048,512]{1,0:T(8,128)(2,1)} fusion(bf16[1024,512]{1,0:T(8,128)(2,1)} %param.18, bf16[1,2048,1024]{2,0,1:T(2,128)(2,1)} %bitcast.137), kind=kOutput, calls=%fused_computation.63 | convolution fusion | flops 2148532224 | bytes 7340032 | tf_op jit(solution)/shard_map/dot_general | solution.py:102
  241.9 6.1 %reshape.221 = bf16[4,4,128,8,64]{4,3,2,1,0:T(8,128)(2,1)} reshape(bf16[2048,512]{1,0:T(8,128)(2,1)} %fusion.62) | data formatting | bytes 4194304 | tf_op jit(solution)/shard_map/reshape;reshape;reshape | solution.py:37
  248.1 5.1 copy.39
  253.1 66.6 %collective-permute-done = bf16[2,16,128,512]{2,3,1,0:T(8,128)(2,1)} collective-permute-done((bf16[2,16,128,512]{2,3,1,0:T(8,128)(2,1)}, bf16[2,16,128,512]{2,3,1,0:T(8,128)(2,1)}, u32[]{:S(2)}, u32[]{:S(2)}) %collective-permute-start) | collective-permute-done | bytes 4194336 | tf_op jit(solution)/shard_map/ppermute | solution.py:18
  319.7 6.3 %pad_maximum_fusion = bf16[2,16,384,512]{2,3,1,0:T(8,128)(2,1)S(1)} fusion(bf16[2,16,128,512]{2,3,1,0:T(8,128)(2,1)} %collective-permute-done.1, bf16[1,16,128,512]{2,3,1,0:T(8,128)(2,1)} %copy.37, bf16[1,16,128,512]{2,3,1,0:T(8,128)(2,1)S(1)} %copy.36, bf16[2,16,128,512]{2,3,1,0:T(8,128)(2,1)} %collective-permute-done), kind=kLoop, calls=%fused_computation.47 | loop fusion | flops 50331648 | bytes 25165824 | tf_op jit(solution)/shard_map/concatenate | solution.py:20
  326.1 5.9 %fusion.81 = (bf16[1,16,384,512]{2,3,1,0:T(8,128)(2,1)}, bf16[1,16,384,512]{2,3,1,0:T(8,128)(2,1)}) fusion(bf16[2,16,384,512]{2,3,1,0:T(8,128)(2,1)S(1)} %pad_maximum_fusion), kind=kLoop, calls=%fused_computation.83 | loop fusion | bytes 25165824 | tf_op jit(solution)/shard_map/slice | solution.py:116
  332.0 70.7 %while.13 = (s32[]{:T(128)}, bf16[4,4,384,8,64]{2,4,3,1,0:T(8,128)(2,1)}, bf16[4,4,384,8,64]{2,4,3,1,0:T(8,128)(2,1)}, bf16[4,4,128,8,64]{2,4,3,1,0:T(8,128)(2,1...) while((s32[]{:T(128)}, ...), condition=%wide.region_4.5_spmd.clone, body=%wide.region_1.0_spmd.clone.sunk | while | flops 1044111360 | bytes 75687264 | solution.py:41
  332.1 2.8 fusion.102
  334.9 2.3 exponential_reduce_fusion.2
  337.2 2.8 bitcast_dynamic-update-slice_fusion.5
  340.1 3.4 fusion.103
  343.5 6.2 %bitcast_dynamic-update-slice_fusion.4 = bf16[4,4,384,8,64]{2,4,3,1,0:T(8,128)(2,1)} fusion(bf16[4,4,384,8,64]{2,4,3,1,0:T(8,128)(2,1)} %get-tuple-element.211, s32[]{:T(128)} %get-tuple-element.210, f32[4,8,128,384]{3,2,1,0:T(8,128)} %copy-done.2, f32[4,8,128]{2,1,0:T(8,128)S(1)} %fusion.103, f32[4,8,128]{2,1,0:T(8,128)S(1)} %log_add_fusion.2, ...), kind=kOutput, calls=%fused_computation.14.clone.1 | convolution fusion | flops 414449664 | bytes 10521600 | tf_op jit(solution)/shard_map/while/body/eval_jaxpr/shij,sihd->sjhd/dot_general | solution.py:68
  349.7 2.8 fusion.102
  352.5 2.3 exponential_reduce_fusion.2
  354.9 2.8 bitcast_dynamic-update-slice_fusion.5
  357.7 3.4 fusion.103
  361.2 6.2 %bitcast_dynamic-update-slice_fusion.4 = bf16[4,4,384,8,64]{2,4,3,1,0:T(8,128)(2,1)} fusion(bf16[4,4,384,8,64]{2,4,3,1,0:T(8,128)(2,1)} %get-tuple-element.211, s32[]{:T(128)} %get-tuple-element.210, f32[4,8,128,384]{3,2,1,0:T(8,128)} %copy-done.2, f32[4,8,128]{2,1,0:T(8,128)S(1)} %fusion.103, f32[4,8,128]{2,1,0:T(8,128)S(1)} %log_add_fusion.2, ...), kind=kOutput, calls=%fused_computation.14.clone.1 | convolution fusion | flops 414449664 | bytes 10521600 | tf_op jit(solution)/shard_map/while/body/eval_jaxpr/shij,sihd->sjhd/dot_general | solution.py:68
  367.4 2.8 fusion.102
  370.2 2.3 exponential_reduce_fusion.2
  372.6 2.9 bitcast_dynamic-update-slice_fusion.5
  375.5 3.4 fusion.103
  378.9 6.2 %bitcast_dynamic-update-slice_fusion.4 = bf16[4,4,384,8,64]{2,4,3,1,0:T(8,128)(2,1)} fusion(bf16[4,4,384,8,64]{2,4,3,1,0:T(8,128)(2,1)} %get-tuple-element.211, s32[]{:T(128)} %get-tuple-element.210, f32[4,8,128,384]{3,2,1,0:T(8,128)} %copy-done.2, f32[4,8,128]{2,1,0:T(8,128)S(1)} %fusion.103, f32[4,8,128]{2,1,0:T(8,128)S(1)} %log_add_fusion.2, ...), kind=kOutput, calls=%fused_computation.14.clone.1 | convolution fusion | flops 414449664 | bytes 10521600 | tf_op jit(solution)/shard_map/while/body/eval_jaxpr/shij,sihd->sjhd/dot_general | solution.py:68
  385.1 2.8 fusion.102
  387.9 2.3 exponential_reduce_fusion.2
  390.3 2.8 bitcast_dynamic-update-slice_fusion.5
  393.1 3.4 fusion.103
  396.6 6.2 %bitcast_dynamic-update-slice_fusion.4 = bf16[4,4,384,8,64]{2,4,3,1,0:T(8,128)(2,1)} fusion(bf16[4,4,384,8,64]{2,4,3,1,0:T(8,128)(2,1)} %get-tuple-element.211, s32[]{:T(128)} %get-tuple-element.210, f32[4,8,128,384]{3,2,1,0:T(8,128)} %copy-done.2, f32[4,8,128]{2,1,0:T(8,128)S(1)} %fusion.103, f32[4,8,128]{2,1,0:T(8,128)S(1)} %log_add_fusion.2, ...), kind=kOutput, calls=%fused_computation.14.clone.1 | convolution fusion | flops 414449664 | bytes 10521600 | tf_op jit(solution)/shard_map/while/body/eval_jaxpr/shij,sihd->sjhd/dot_general | solution.py:68
  402.7 4.0 fusion.54
  406.7 2.6 collective-permute-start.2
  409.3 3.5 collective-permute-start.3
  412.8 88.9 %collective-permute-done.2 = bf16[2,16,128,512]{2,3,1,0:T(8,128)(2,1)S(1)} collective-permute-done((bf16[2,16,128,512]{2,3,1,0:T(8,128)(2,1)S(1)}, bf16[2,16,128,512]{2,3,1,0:T(8,128)(2,1)S(1)}, u32[]{:S(2)}, u32[]{:S(2)}) %collective-permute-start.2) | collective-permute-done | bytes 4194336 | tf_op jit(solution)/shard_map/ppermute | solution.py:27
  505.4 3.9 copy.40
  509.3 2.6 copy.41
  (58 shorter events, 8.1 us)
Async XLA Ops:
  0.6 198.7 %copy-start = (bf16[1024,512]{1,0:T(8,128)(2,1)S(1)}, bf16[1024,512]{1,0:T(8,128)(2,1)}, u32[]{:S(2)}) copy-start(bf16[1024,512]{1,0:T(8,128)(2,1)} %param.19) | copy-start | bytes 3145732
  2.8 13.7 %copy-start.8 = (bf16[24,1024]{1,0:T(8,128)(2,1)S(1)}, bf16[24,1024]{1,0:T(8,128)(2,1)}, u32[]{:S(2)}) copy-start(bf16[24,1024]{1,0:T(8,128)(2,1)} %param.15) | copy-start | bytes 147460
  2.8 17.5 %copy-start.9 = (f32[1024]{0:T(1024)S(1)}, f32[1024]{0:T(1024)}, u32[]{:S(2)}) copy-start(f32[1024]{0:T(1024)} %param.16) | copy-start | bytes 12292
  16.5 3.8 copy-start.3
  220.7 13.7 %copy-start.10 = (s32[16,3]{0,1:T(4,128)S(1)}, s32[16,3]{0,1:T(4,128)}, u32[]{:S(2)}) copy-start(s32[16,3]{0,1:T(4,128)} %param.22) | copy-start | bytes 580
  220.7 13.9 %copy-start.11 = (f32[8]{0:T(128)S(1)}, f32[8]{0:T(128)}, u32[]{:S(2)}) copy-start(f32[8]{0:T(128)} %param.21) | copy-start | bytes 100
  224.7 95.1 %collective-permute-start = (bf16[2,16,128,512]{2,3,1,0:T(8,128)(2,1)}, bf16[2,16,128,512]{2,3,1,0:T(8,128)(2,1)}, u32[]{:S(2)}, u32[]{:S(2)}) collective-permute-start(bf16[2,16,128,512]{2,3,1,0:T(8,128)(2,1)} %pad_maximum_fusion.2), channel_id=1, source_target_pairs={{0,1},{1,2},{2,3},{3,4},{4,5},{5,6},{6,7},{7,8},{8,9},{9,10},{10,1... | collective-permute-start | bytes 12582920 | tf_op jit(solution)/shard_map/ppermute | solution.py:18
  226.9 92.9 %collective-permute-start.1 = (bf16[2,16,128,512]{2,3,1,0:T(8,128)(2,1)}, bf16[2,16,128,512]{2,3,1,0:T(8,128)(2,1)}, u32[]{:S(2)}, u32[]{:S(2)}) collective-permute-start(bf16[2,16,128,512]{2,3,1,0:T(8,128)(2,1)} %pad_maximum_fusion.2), channel_id=1, source_target_pairs={{1,0},{2,1},{3,2},{4,3},{5,4},{6,5},{7,6},{8,7},{9,8},{10,9},{11,1... | collective-permute-start | bytes 12582920 | tf_op jit(solution)/shard_map/ppermute | solution.py:19
  326.1 6.0 %copy-start.6 = (bf16[4,4,128,8,64]{2,4,3,1,0:T(8,128)(2,1)S(1)}, bf16[4,4,128,8,64]{2,4,3,1,0:T(8,128)(2,1)}, u32[]{:S(2)}) copy-start(bf16[4,4,128,8,64]{2,4,3,1,0:T(8,128)(2,1)} %copy.39) | copy-start | bytes 6291460
  332.1 5.1 %copy-start.7 = (bf16[4,4,128,8,64]{2,4,3,1,0:T(8,128)(2,1)S(1)}, bf16[4,4,128,8,64]{2,4,3,1,0:T(8,128)(2,1)}, u32[]{:S(2)}) copy-start(bf16[4,4,128,8,64]{2,4,3,1,0:T(8,128)(2,1)} %get-tuple-element.226) | copy-start | bytes 6291460 | tf_op jit(solution)/shard_map/while
  334.9 5.2 %copy-start.2 = (f32[4,8,128,384]{3,2,1,0:T(8,128)}, f32[4,8,128,384]{3,2,1,0:T(8,128)S(1)}, u32[]{:S(2)}) copy-start(f32[4,8,128,384]{3,2,1,0:T(8,128)S(1)} %get-tuple-element.198) | copy-start | bytes 18874372 | tf_op jit(solution)/shard_map/while
  349.7 5.1 %copy-start.7 = (bf16[4,4,128,8,64]{2,4,3,1,0:T(8,128)(2,1)S(1)}, bf16[4,4,128,8,64]{2,4,3,1,0:T(8,128)(2,1)}, u32[]{:S(2)}) copy-start(bf16[4,4,128,8,64]{2,4,3,1,0:T(8,128)(2,1)} %get-tuple-element.226) | copy-start | bytes 6291460 | tf_op jit(solution)/shard_map/while
  352.5 5.2 %copy-start.2 = (f32[4,8,128,384]{3,2,1,0:T(8,128)}, f32[4,8,128,384]{3,2,1,0:T(8,128)S(1)}, u32[]{:S(2)}) copy-start(f32[4,8,128,384]{3,2,1,0:T(8,128)S(1)} %get-tuple-element.198) | copy-start | bytes 18874372 | tf_op jit(solution)/shard_map/while
  367.4 5.1 %copy-start.7 = (bf16[4,4,128,8,64]{2,4,3,1,0:T(8,128)(2,1)S(1)}, bf16[4,4,128,8,64]{2,4,3,1,0:T(8,128)(2,1)}, u32[]{:S(2)}) copy-start(bf16[4,4,128,8,64]{2,4,3,1,0:T(8,128)(2,1)} %get-tuple-element.226) | copy-start | bytes 6291460 | tf_op jit(solution)/shard_map/while
  370.2 5.2 %copy-start.2 = (f32[4,8,128,384]{3,2,1,0:T(8,128)}, f32[4,8,128,384]{3,2,1,0:T(8,128)S(1)}, u32[]{:S(2)}) copy-start(f32[4,8,128,384]{3,2,1,0:T(8,128)S(1)} %get-tuple-element.198) | copy-start | bytes 18874372 | tf_op jit(solution)/shard_map/while
  385.1 5.1 %copy-start.7 = (bf16[4,4,128,8,64]{2,4,3,1,0:T(8,128)(2,1)S(1)}, bf16[4,4,128,8,64]{2,4,3,1,0:T(8,128)(2,1)}, u32[]{:S(2)}) copy-start(bf16[4,4,128,8,64]{2,4,3,1,0:T(8,128)(2,1)} %get-tuple-element.226) | copy-start | bytes 6291460 | tf_op jit(solution)/shard_map/while
  387.9 5.2 %copy-start.2 = (f32[4,8,128,384]{3,2,1,0:T(8,128)}, f32[4,8,128,384]{3,2,1,0:T(8,128)S(1)}, u32[]{:S(2)}) copy-start(f32[4,8,128,384]{3,2,1,0:T(8,128)S(1)} %get-tuple-element.198) | copy-start | bytes 18874372 | tf_op jit(solution)/shard_map/while
  402.7 99.0 %copy-start.4 = (bf16[4,4,384,8,64]{2,4,3,1,0:T(8,128)(2,1)S(1)}, bf16[4,4,384,8,64]{2,4,3,1,0:T(8,128)(2,1)}, u32[]{:S(2)}) copy-start(bf16[4,4,384,8,64]{2,4,3,1,0:T(8,128)(2,1)} %get-tuple-element.50) | copy-start | bytes 18874372
  402.7 99.0 %copy-start.5 = (bf16[4,4,384,8,64]{2,4,3,1,0:T(8,128)(2,1)S(1)}, bf16[4,4,384,8,64]{2,4,3,1,0:T(8,128)(2,1)}, u32[]{:S(2)}) copy-start(bf16[4,4,384,8,64]{2,4,3,1,0:T(8,128)(2,1)} %get-tuple-element.51) | copy-start | bytes 18874372
  406.7 95.0 %collective-permute-start.2 = (bf16[2,16,128,512]{2,3,1,0:T(8,128)(2,1)S(1)}, bf16[2,16,128,512]{2,3,1,0:T(8,128)(2,1)S(1)}, u32[]{:S(2)}, u32[]{:S(2)}) collective-permute-start(bf16[2,16,128,512]{2,3,1,0:T(8,128)(2,1)S(1)} %get-tuple-element.135), channel_id=1, source_target_pairs={{0,1},{1,2},{2,3},{3,4},{4,5},{5,6},{6,7},{7,8},{8,9},{9,10},{10,1... | collective-permute-start | bytes 12582920 | tf_op jit(solution)/shard_map/ppermute | solution.py:27
  409.3 92.4 %collective-permute-start.3 = (bf16[2,16,128,512]{2,3,1,0:T(8,128)(2,1)S(1)}, bf16[2,16,128,512]{2,3,1,0:T(8,128)(2,1)S(1)}, u32[]{:S(2)}, u32[]{:S(2)}) collective-permute-start(bf16[2,16,128,512]{2,3,1,0:T(8,128)(2,1)S(1)} %get-tuple-element.136), channel_id=1, source_target_pairs={{1,0},{2,1},{3,2},{4,3},{5,4},{6,5},{7,6},{8,7},{9,8},{10,9},{11,1... | collective-permute-start | bytes 12582920 | tf_op jit(solution)/shard_map/ppermute | solution.py:27
  503.7 8.2 %copy-start.1 = (bf16[1024,512]{1,0:T(8,128)(2,1)S(1)}, bf16[1024,512]{1,0:T(8,128)(2,1)}, u32[]{:S(2)}) copy-start(bf16[1024,512]{1,0:T(8,128)(2,1)} %param.19) | copy-start | bytes 3145732
where the time goes:
time: 513 us; the launch traced here: 512 us
  waiting for transfers between devices  156 us (30%)
  local copies, waits for them, and re-layouts  103 us (20%)
  blocking collectives  98.4 us (19%)
  matrix products  82.8 us (16%)
  other arithmetic  58.4 us (11%)
  starting transfers between devices  11.9 us (2%)
    all_to_all x1, blocking collectives, on_device(): lax.all_to_all(normed, 'bus', split_axis=1, concat_axis=0, tiled=True)  98.4 us
    ppermute x2, waiting for transfers between devices, from_behind(): lax.ppermute(value, axis, [(source, source + steps) for source in range(l...  88.9 us
    ppermute x1, waiting for transfers between devices, with_halo(): before = lax.ppermute(last, axis, up)  66.6 us
    unnamed x27, local copies, waits for them, and re-layouts  39.7 us
    convert_element_type x1, local copies, waits for them, and re-layouts, on_device(): normed = (mixed * lax.rsqrt(jnp.mean(mixed * mixed, axis=-1, keepdims=Tru...  28.7 us
    unnamed x1, other arithmetic  25.9 us
    dot_general x4, matrix products, reader_terms(): jnp.einsum('shij,sihd->sjhd', dscores, queries, preferred_element_type=jn...  24.6 us
    dot_general x3, matrix products, on_device(): jnp.dot(flat_rows, weight, preferred_element_type=jnp.float32)  21.8 us
  transfers between devices with their start and end apart: 4, of which 2 were waited for; matrix products, arithmetic and copies ran while one was open for 4% of the time, Pallas kernels for 0%

commit v1 on v0

--- a/solution.py
+++ b/solution.py
@@ -6,6 +6,22 @@
 
 EPSILON = 1e-05
 NEG_FILL = -1e30
+
+
+def pairwise_exchange(array, axis, split, join):
+    ways, here = (lax.axis_size(axis), lax.axis_index(axis))
+    width = array.shape[split] // ways
+    lengths = list(array.shape)
+    lengths[split] = width
+    height = lengths[join]
+    lengths[join] = height * ways
+    full = jnp.zeros(lengths, array.dtype)
+    for mask in range(ways):
+        part = lax.dynamic_slice_in_dim(array, (here ^ mask) * width, width, axis=split)
+        if mask:
+            part = lax.ppermute(part, axis, [(d, d ^ mask) for d in range(ways)])
+        full = lax.dynamic_update_slice_in_dim(full, part, (here ^ mask) * height, axis=join)
+    return full
 
 
 def with_halo(shard, sides, width):
@@ -96,7 +112,7 @@
     normed = (
         mixed * lax.rsqrt(jnp.mean(mixed * mixed, axis=-1, keepdims=True) + EPSILON) * norm_gain
     ).astype(jnp.bfloat16)
-    arrived = lax.all_to_all(normed, "bus", split_axis=1, concat_axis=0, tiled=True)
+    arrived = pairwise_exchange(normed, "bus", 1, 0)
     flat_rows = arrived.reshape(-1, arrived.shape[2])
     queries, key_rows, value_rows = [
         jnp.dot(flat_rows, weight, preferred_element_type=jnp.float32)

time: 513 us -> 450 us (0.88)
  blocking collectives: 98.4 us -> 0 us
  waiting for transfers between devices: 156 us -> 238 us
  local copies, waits for them, and re-layouts: 103 us -> 73.2 us
  other arithmetic: 58.4 us -> 33.8 us
  starting transfers between devices: 11.9 us -> 23.5 us
    all_to_all x1 -> x0, blocking collectives: 98.4 us -> none  [on_device(): lax.all_to_all(normed, 'bus', split_axis=1, concat_axis=0, tiled=True)]
    ppermute x0 -> x15, waiting for transfers between devices: none -> 80.9 us  [pairwise_exchange(): part = lax.ppermute(part, axis, [(d, d ^ mask) for d in range(ways)])]
    convert_element_type x1 -> x0, local copies, waits for them, and re-layouts: 28.7 us -> none  [on_device(): normed = (mixed * lax.rsqrt(jnp.mean(mixed * mixed, axis=-1, keepdims=Tru...]
    unnamed x1 -> x2, other arithmetic: 25.9 us -> 0.01 us
    unnamed x27 -> x30, local copies, waits for them, and re-layouts: 39.7 us -> 17.6 us
    dynamic_update_slice x0 -> x15, local copies, waits for them, and re-layouts: none -> 15.6 us  [pairwise_exchange(): lax.dynamic_update_slice_in_dim(full, part, (here ^ mask) * height, axis=...]
    ppermute x0 -> x15, starting transfers between devices: none -> 11.5 us  [pairwise_exchange(): part = lax.ppermute(part, axis, [(d, d ^ mask) for d in range(ways)])]
  transfers between devices with their start and end apart: 4 -> 19, of which waited for: 2 -> 13; matrix products, arithmetic and copies ran while one was open for 4% -> 8% of each run, Pallas kernels for 0% -> 0%
where the time goes in v1:
time: 450 us; the launch traced here: 448 us
  waiting for transfers between devices  238 us (53%)
  matrix products  78.2 us (17%)
  local copies, waits for them, and re-layouts  73.2 us (16%)
  other arithmetic  33.8 us (8%)
  starting transfers between devices  23.5 us (5%)
    ppermute x2, waiting for transfers between devices, from_behind(): lax.ppermute(value, axis, [(source, source + steps) for source in range(l...  89 us
    ppermute x15, waiting for transfers between devices, pairwise_exchange(): part = lax.ppermute(part, axis, [(d, d ^ mask) for d in range(ways)])  80.9 us
    ppermute x1, waiting for transfers between devices, with_halo(): before = lax.ppermute(last, axis, up)  67.7 us
    dot_general x4, matrix products, reader_terms(): jnp.einsum('shij,sihd->sjhd', dscores, queries, preferred_element_type=jn...  24.7 us
    dot_general x3, matrix products, on_device(): jnp.dot(flat_rows, weight, preferred_element_type=jnp.float32)  17.8 us
    unnamed x30, local copies, waits for them, and re-layouts  17.6 us
    dynamic_update_slice x15, local copies, waits for them, and re-layouts, pairwise_exchange(): lax.dynamic_update_slice_in_dim(full, part, (here ^ mask) * height, axis=...  15.6 us
    dot_general x4, matrix products, reader_terms(): jnp.einsum('shij,sjhd->sihd', weights_b, value_tiles, preferred_element_t...  13.8 us
  transfers between devices with their start and end apart: 19, of which 13 were waited for; matrix products, arithmetic and copies ran while one was open for 8% of the time, Pallas kernels for 0%

profile of v1, /device:TPU:12, one launch (start us, length us, event | category | flops | bytes accessed | tf_op | source)
XLA Modules:
  0.0 448.2 jit_solution(12296448772029070610)
XLA Ops:
  2.9 13.7 %gather_fusion = bf16[2048,1024]{1,0:T(8,128)(2,1)} fusion(bf16[2048,1024]{1,0:T(8,128)(2,1)} %bitcast.116, s32[2048]{0:T(1024)S(1)} %fusion.56), kind=kCustom, calls=%fused_computation | custom fusion | bytes 8396800 | tf_op jit(solution)/shard_map/jit(_take)/gather | solution.py:106
  16.7 3.4 multiply_reduce_fusion
  20.2 3.3 multiply_convert_fusion.6
  33.2 3.9 collective-permute-done.1
  38.8 3.2 collective-permute-done.2
  41.9 2.6 collective-permute-start.7
  52.3 7.2 %collective-permute-done.5 = bf16[1,128,1024]{2,1,0:T(8,128)(2,1)S(1)} collective-permute-done((bf16[1,128,1024]{2,1,0:T(8,128)(2,1)}, bf16[1,128,1024]{2,1,0:T(8,128)(2,1)S(1)}, u32[]{:S(2)}, u32[]{:S(2)}) %collective-permute-start.5) | collective-permute-done | bytes 262176 | tf_op jit(solution)/shard_map/ppermute | solution.py:22
  66.6 24.0 %collective-permute-done.8 = bf16[1,128,1024]{2,1,0:T(8,128)(2,1)S(1)} collective-permute-done((bf16[1,128,1024]{2,1,0:T(8,128)(2,1)S(1)}, bf16[1,128,1024]{2,1,0:T(8,128)(2,1)S(1)}, u32[]{:S(2)}, u32[]{:S(2)}) %collective-permute-start.8) | collective-permute-done | bytes 262176 | tf_op jit(solution)/shard_map/ppermute | solution.py:22
  91.2 10.5 %collective-permute-done.9 = bf16[1,128,1024]{2,1,0:T(8,128)(2,1)S(1)} collective-permute-done((bf16[1,128,1024]{2,1,0:T(8,128)(2,1)S(1)}, bf16[1,128,1024]{2,1,0:T(8,128)(2,1)S(1)}, u32[]{:S(2)}, u32[]{:S(2)}) %collective-permute-start.9) | collective-permute-done | bytes 262176 | tf_op jit(solution)/shard_map/ppermute | solution.py:22
  102.5 4.8 %collective-permute-done.10 = bf16[1,128,1024]{2,1,0:T(8,128)(2,1)S(1)} collective-permute-done((bf16[1,128,1024]{2,1,0:T(8,128)(2,1)S(1)}, bf16[1,128,1024]{2,1,0:T(8,128)(2,1)S(1)}, u32[]{:S(2)}, u32[]{:S(2)}) %collective-permute-start.10) | collective-permute-done | bytes 262176 | tf_op jit(solution)/shard_map/ppermute | solution.py:22
  108.0 10.6 %collective-permute-done.11 = bf16[1,128,1024]{2,1,0:T(8,128)(2,1)S(1)} collective-permute-done((bf16[1,128,1024]{2,1,0:T(8,128)(2,1)S(1)}, bf16[1,128,1024]{2,1,0:T(8,128)(2,1)S(1)}, u32[]{:S(2)}, u32[]{:S(2)}) %collective-permute-start.11) | collective-permute-done | bytes 262176 | tf_op jit(solution)/shard_map/ppermute | solution.py:22
  119.3 4.9 %collective-permute-done.12 = bf16[1,128,1024]{2,1,0:T(8,128)(2,1)S(1)} collective-permute-done((bf16[1,128,1024]{2,1,0:T(8,128)(2,1)S(1)}, bf16[1,128,1024]{2,1,0:T(8,128)(2,1)S(1)}, u32[]{:S(2)}, u32[]{:S(2)}) %collective-permute-start.12) | collective-permute-done | bytes 262176 | tf_op jit(solution)/shard_map/ppermute | solution.py:22
  124.9 4.9 %collective-permute-done.13 = bf16[1,128,1024]{2,1,0:T(8,128)(2,1)S(1)} collective-permute-done((bf16[1,128,1024]{2,1,0:T(8,128)(2,1)S(1)}, bf16[1,128,1024]{2,1,0:T(8,128)(2,1)S(1)}, u32[]{:S(2)}, u32[]{:S(2)}) %collective-permute-start.13) | collective-permute-done | bytes 262176 | tf_op jit(solution)/shard_map/ppermute | solution.py:22
  130.6 4.5 %collective-permute-done.14 = bf16[1,128,1024]{2,1,0:T(8,128)(2,1)S(1)} collective-permute-done((bf16[1,128,1024]{2,1,0:T(8,128)(2,1)S(1)}, bf16[1,128,1024]{2,1,0:T(8,128)(2,1)S(1)}, u32[]{:S(2)}, u32[]{:S(2)}) %collective-permute-start.14) | collective-permute-done | bytes 262176 | tf_op jit(solution)/shard_map/ppermute | solution.py:22
  135.8 5.8 %convolution_convert_fusion.2 = bf16[2048,512]{1,0:T(8,128)(2,1)} fusion(bf16[2048,1024]{1,0:T(8,128)(2,1)} %bitcast.127, bf16[1024,512]{1,0:T(8,128)(2,1)S(1)} %copy-done), kind=kOutput, calls=%fused_computation.58 | convolution fusion | flops 2148532224 | bytes 7340032 | tf_op jit(solution)/shard_map/dot_general | solution.py:118
  141.6 3.1 copy.19
  144.8 5.8 %convolution_convert_fusion.1 = bf16[2048,512]{1,0:T(8,128)(2,1)} fusion(bf16[2048,1024]{1,0:T(8,128)(2,1)} %bitcast.128, bf16[1024,512]{1,0:T(8,128)(2,1)S(1)} %copy-done.9), kind=kOutput, calls=%fused_computation.57 | convolution fusion | flops 2148532224 | bytes 7340032 | tf_op jit(solution)/shard_map/dot_general | solution.py:118
  150.6 3.9 copy.20
  154.5 3.9 pad_maximum_fusion.2
  160.5 3.8 collective-permute-start.16
  164.4 3.9 copy.21
  168.5 6.1 %convolution_convert_fusion.3 = bf16[2048,512]{1,0:T(8,128)(2,1)} fusion(bf16[2048,1024]{1,0:T(8,128)(2,1)} %bitcast.129, bf16[1024,512]{1,0:T(8,128)(2,1)} %param.18), kind=kOutput, calls=%fused_computation.59 | convolution fusion | flops 2148532224 | bytes 7340032 | tf_op jit(solution)/shard_map/dot_general | solution.py:118
  174.6 6.3 %reshape.217 = bf16[4,4,128,8,64]{4,3,2,1,0:T(8,128)(2,1)} reshape(bf16[2048,512]{1,0:T(8,128)(2,1)} %convolution_convert_fusion.3) | data formatting | bytes 4194304 | tf_op jit(solution)/shard_map/reshape;reshape;reshape | solution.py:53
  180.9 5.1 %copy.22 = bf16[4,4,128,8,64]{2,4,3,1,0:T(8,128)(2,1)} copy(bf16[4,4,128,8,64]{4,3,2,1,0:T(8,128)(2,1)} %reshape.217) | data formatting | bytes 4194304
  186.0 67.7 %collective-permute-done.15 = bf16[2,16,128,512]{2,3,1,0:T(8,128)(2,1)} collective-permute-done((bf16[2,16,128,512]{2,3,1,0:T(8,128)(2,1)}, bf16[2,16,128,512]{2,3,1,0:T(8,128)(2,1)}, u32[]{:S(2)}, u32[]{:S(2)}) %collective-permute-start.15) | collective-permute-done | bytes 4194336 | tf_op jit(solution)/shard_map/ppermute | solution.py:34
  253.7 6.3 %pad_maximum_fusion = bf16[2,16,384,512]{2,3,1,0:T(8,128)(2,1)S(1)} fusion(bf16[2,16,128,512]{2,3,1,0:T(8,128)(2,1)} %collective-permute-done.16, bf16[1,16,128,512]{2,3,1,0:T(8,128)(2,1)} %copy.20, bf16[1,16,128,512]{2,3,1,0:T(8,128)(2,1)S(1)} %copy.19, bf16[2,16,128,512]{2,3,1,0:T(8,128)(2,1)} %collective-permute-done.15), kind=kLoop, calls=%fused_computation.47 | loop fusion | flops 50331648 | bytes 25165824 | tf_op jit(solution)/shard_map/concatenate | solution.py:36
  260.0 5.8 %fusion.64 = (bf16[1,16,384,512]{2,3,1,0:T(8,128)(2,1)}, bf16[1,16,384,512]{2,3,1,0:T(8,128)(2,1)}) fusion(bf16[2,16,384,512]{2,3,1,0:T(8,128)(2,1)S(1)} %pad_maximum_fusion), kind=kLoop, calls=%fused_computation.106 | loop fusion | bytes 25165824 | tf_op jit(solution)/shard_map/slice | solution.py:132
  265.8 73.2 %while.13 = (s32[]{:T(128)}, bf16[4,4,384,8,64]{2,4,3,1,0:T(8,128)(2,1)}, bf16[4,4,384,8,64]{2,4,3,1,0:T(8,128)(2,1)}, bf16[4,4,128,8,64]{2,4,3,1,0:T(8,128)(2,1...) while((s32[]{:T(128)}, ...), condition=%wide.region_4.5_spmd.clone, body=%wide.region_1.0_spmd.clone.sunk | while | flops 1044111360 | bytes 75687264 | solution.py:57
  265.8 2.6 fusion.88
  271.6 2.8 bitcast_dynamic-update-slice_fusion.5
  274.4 3.4 fusion.89
  277.9 6.2 %bitcast_dynamic-update-slice_fusion.4 = bf16[4,4,384,8,64]{2,4,3,1,0:T(8,128)(2,1)} fusion(bf16[4,4,384,8,64]{2,4,3,1,0:T(8,128)(2,1)} %get-tuple-element.205, s32[]{:T(128)} %get-tuple-element.204, f32[4,8,128,384]{3,2,1,0:T(8,128)} %copy-done.2, f32[4,8,128]{2,1,0:T(8,128)S(1)} %fusion.89, f32[4,8,128]{2,1,0:T(8,128)S(1)} %log_add_fusion.2, ...), kind=kOutput, calls=%fused_computation.17.clone.1 | convolution fusion | flops 414449664 | bytes 10521600 | tf_op jit(solution)/shard_map/while/body/eval_jaxpr/shij,sihd->sjhd/dot_general | solution.py:84
  284.1 2.6 fusion.88
  289.9 2.8 bitcast_dynamic-update-slice_fusion.5
  292.7 3.4 fusion.89
  296.1 6.2 %bitcast_dynamic-update-slice_fusion.4 = bf16[4,4,384,8,64]{2,4,3,1,0:T(8,128)(2,1)} fusion(bf16[4,4,384,8,64]{2,4,3,1,0:T(8,128)(2,1)} %get-tuple-element.205, s32[]{:T(128)} %get-tuple-element.204, f32[4,8,128,384]{3,2,1,0:T(8,128)} %copy-done.2, f32[4,8,128]{2,1,0:T(8,128)S(1)} %fusion.89, f32[4,8,128]{2,1,0:T(8,128)S(1)} %log_add_fusion.2, ...), kind=kOutput, calls=%fused_computation.17.clone.1 | convolution fusion | flops 414449664 | bytes 10521600 | tf_op jit(solution)/shard_map/while/body/eval_jaxpr/shij,sihd->sjhd/dot_general | solution.py:84
  302.4 2.6 fusion.88
  308.2 2.8 bitcast_dynamic-update-slice_fusion.5
  311.0 3.4 fusion.89
  314.4 6.2 %bitcast_dynamic-update-slice_fusion.4 = bf16[4,4,384,8,64]{2,4,3,1,0:T(8,128)(2,1)} fusion(bf16[4,4,384,8,64]{2,4,3,1,0:T(8,128)(2,1)} %get-tuple-element.205, s32[]{:T(128)} %get-tuple-element.204, f32[4,8,128,384]{3,2,1,0:T(8,128)} %copy-done.2, f32[4,8,128]{2,1,0:T(8,128)S(1)} %fusion.89, f32[4,8,128]{2,1,0:T(8,128)S(1)} %log_add_fusion.2, ...), kind=kOutput, calls=%fused_computation.17.clone.1 | convolution fusion | flops 414449664 | bytes 10521600 | tf_op jit(solution)/shard_map/while/body/eval_jaxpr/shij,sihd->sjhd/dot_general | solution.py:84
  320.7 2.6 fusion.88
  326.5 2.8 bitcast_dynamic-update-slice_fusion.5
  329.3 3.4 fusion.89
  332.8 6.2 %bitcast_dynamic-update-slice_fusion.4 = bf16[4,4,384,8,64]{2,4,3,1,0:T(8,128)(2,1)} fusion(bf16[4,4,384,8,64]{2,4,3,1,0:T(8,128)(2,1)} %get-tuple-element.205, s32[]{:T(128)} %get-tuple-element.204, f32[4,8,128,384]{3,2,1,0:T(8,128)} %copy-done.2, f32[4,8,128]{2,1,0:T(8,128)S(1)} %fusion.89, f32[4,8,128]{2,1,0:T(8,128)S(1)} %log_add_fusion.2, ...), kind=kOutput, calls=%fused_computation.17.clone.1 | convolution fusion | flops 414449664 | bytes 10521600 | tf_op jit(solution)/shard_map/while/body/eval_jaxpr/shij,sihd->sjhd/dot_general | solution.py:84
  338.9 4.0 fusion.54
  345.3 3.7 collective-permute-start.18
  349.0 89.0 %collective-permute-done.17 = bf16[2,16,128,512]{2,3,1,0:T(8,128)(2,1)S(1)} collective-permute-done((bf16[2,16,128,512]{2,3,1,0:T(8,128)(2,1)S(1)}, bf16[2,16,128,512]{2,3,1,0:T(8,128)(2,1)S(1)}, u32[]{:S(2)}, u32[]{:S(2)}) %collective-permute-start.17) | collective-permute-done | bytes 4194336 | tf_op jit(solution)/shard_map/ppermute | solution.py:43
  441.6 4.0 copy.24
  (107 shorter events, 56.3 us)
Async XLA Ops:
  0.6 135.2 %copy-start = (bf16[1024,512]{1,0:T(8,128)(2,1)S(1)}, bf16[1024,512]{1,0:T(8,128)(2,1)}, u32[]{:S(2)}) copy-start(bf16[1024,512]{1,0:T(8,128)(2,1)} %param.19) | copy-start | bytes 3145732
  2.9 13.7 %copy-start.6 = (bf16[24,1024]{1,0:T(8,128)(2,1)S(1)}, bf16[24,1024]{1,0:T(8,128)(2,1)}, u32[]{:S(2)}) copy-start(bf16[24,1024]{1,0:T(8,128)(2,1)} %param.15) | copy-start | bytes 147460
  16.6 3.6 copy-start.7
  25.7 2.0 copy-start.4
  27.7 3.5 collective-permute-start
  27.7 9.4 %collective-permute-start.1 = (bf16[1,128,1024]{2,1,0:T(8,128)(2,1)}, bf16[1,128,1024]{2,1,0:T(8,128)(2,1)}, u32[]{:S(2)}, u32[]{:S(2)}) collective-permute-start(bf16[1,128,1024]{2,1,0:T(8,128)(2,1)} %get-tuple-element.132), channel_id=1, source_target_pairs={{0,2},{1,3},{2,0},{3,1},{4,6},{5,7},{6,4},{7,5},{8,10},{9,11},{10,... | collective-permute-start | bytes 786440 | tf_op jit(solution)/shard_map/ppermute | solution.py:22
  28.2 13.8 %collective-permute-start.2 = (bf16[1,128,1024]{2,1,0:T(8,128)(2,1)}, bf16[1,128,1024]{2,1,0:T(8,128)(2,1)}, u32[]{:S(2)}, u32[]{:S(2)}) collective-permute-start(bf16[1,128,1024]{2,1,0:T(8,128)(2,1)} %get-tuple-element.131), channel_id=1, source_target_pairs={{0,3},{1,2},{2,1},{3,0},{4,7},{5,6},{6,5},{7,4},{8,11},{9,10},{10,... | collective-permute-start | bytes 786440 | tf_op jit(solution)/shard_map/ppermute | solution.py:22
  29.5 16.7 %collective-permute-start.3 = (bf16[1,128,1024]{2,1,0:T(8,128)(2,1)}, bf16[1,128,1024]{2,1,0:T(8,128)(2,1)}, u32[]{:S(2)}, u32[]{:S(2)}) collective-permute-start(bf16[1,128,1024]{2,1,0:T(8,128)(2,1)} %get-tuple-element.130), channel_id=1, source_target_pairs={{0,4},{1,5},{2,6},{3,7},{4,0},{5,1},{6,2},{7,3},{8,12},{9,13},{10,... | collective-permute-start | bytes 786440 | tf_op jit(solution)/shard_map/ppermute | solution.py:22
  30.0 18.1 %collective-permute-start.4 = (bf16[1,128,1024]{2,1,0:T(8,128)(2,1)}, bf16[1,128,1024]{2,1,0:T(8,128)(2,1)}, u32[]{:S(2)}, u32[]{:S(2)}) collective-permute-start(bf16[1,128,1024]{2,1,0:T(8,128)(2,1)} %get-tuple-element.129), channel_id=1, source_target_pairs={{0,5},{1,4},{2,7},{3,6},{4,1},{5,0},{6,3},{7,2},{8,13},{9,12},{10,... | collective-permute-start | bytes 786440 | tf_op jit(solution)/shard_map/ppermute | solution.py:22
  31.2 28.3 %collective-permute-start.5 = (bf16[1,128,1024]{2,1,0:T(8,128)(2,1)}, bf16[1,128,1024]{2,1,0:T(8,128)(2,1)S(1)}, u32[]{:S(2)}, u32[]{:S(2)}) collective-permute-start(bf16[1,128,1024]{2,1,0:T(8,128)(2,1)} %get-tuple-element.128), channel_id=1, source_target_pairs={{0,6},{1,7},{2,4},{3,5},{4,2},{5,3},{6,0},{7,1},{8,14},{9,15},{10,... | collective-permute-start | bytes 786440 | tf_op jit(solution)/shard_map/ppermute | solution.py:22
  37.1 27.2 %collective-permute-start.6 = (bf16[1,128,1024]{2,1,0:T(8,128)(2,1)S(1)}, bf16[1,128,1024]{2,1,0:T(8,128)(2,1)S(1)}, u32[]{:S(2)}, u32[]{:S(2)}) collective-permute-start(bf16[1,128,1024]{2,1,0:T(8,128)(2,1)S(1)} %get-tuple-element.127), channel_id=1, source_target_pairs={{0,7},{1,6},{2,5},{3,4},{4,3},{5,2},{6,1},{7,0},{8,15},{9,14},{10,... | collective-permute-start | bytes 786440 | tf_op jit(solution)/shard_map/ppermute | solution.py:22
  41.9 23.6 %collective-permute-start.7 = (bf16[1,128,1024]{2,1,0:T(8,128)(2,1)S(1)}, bf16[1,128,1024]{2,1,0:T(8,128)(2,1)S(1)}, u32[]{:S(2)}, u32[]{:S(2)}) collective-permute-start(bf16[1,128,1024]{2,1,0:T(8,128)(2,1)S(1)} %get-tuple-element.126), channel_id=1, source_target_pairs={{0,8},{1,9},{2,10},{3,11},{4,12},{5,13},{6,14},{7,15},{8,0},{9,1},... | collective-permute-start | bytes 786440 | tf_op jit(solution)/shard_map/ppermute | solution.py:22
  46.2 44.3 %collective-permute-start.8 = (bf16[1,128,1024]{2,1,0:T(8,128)(2,1)S(1)}, bf16[1,128,1024]{2,1,0:T(8,128)(2,1)S(1)}, u32[]{:S(2)}, u32[]{:S(2)}) collective-permute-start(bf16[1,128,1024]{2,1,0:T(8,128)(2,1)S(1)} %get-tuple-element.125), channel_id=1, source_target_pairs={{0,9},{1,8},{2,11},{3,10},{4,13},{5,12},{6,15},{7,14},{8,1},{9,0},... | collective-permute-start | bytes 786440 | tf_op jit(solution)/shard_map/ppermute | solution.py:22
  48.0 53.7 %collective-permute-start.9 = (bf16[1,128,1024]{2,1,0:T(8,128)(2,1)S(1)}, bf16[1,128,1024]{2,1,0:T(8,128)(2,1)S(1)}, u32[]{:S(2)}, u32[]{:S(2)}) collective-permute-start(bf16[1,128,1024]{2,1,0:T(8,128)(2,1)S(1)} %get-tuple-element.124), channel_id=1, source_target_pairs={{0,10},{1,11},{2,8},{3,9},{4,14},{5,15},{6,12},{7,13},{8,2},{9,3},... | collective-permute-start | bytes 786440 | tf_op jit(solution)/shard_map/ppermute | solution.py:22
  59.4 47.8 %collective-permute-start.10 = (bf16[1,128,1024]{2,1,0:T(8,128)(2,1)S(1)}, bf16[1,128,1024]{2,1,0:T(8,128)(2,1)S(1)}, u32[]{:S(2)}, u32[]{:S(2)}) collective-permute-start(bf16[1,128,1024]{2,1,0:T(8,128)(2,1)S(1)} %get-tuple-element.123), channel_id=1, source_target_pairs={{0,11},{1,10},{2,9},{3,8},{4,15},{5,14},{6,13},{7,12},{8,3},{9,2},... | collective-permute-start | bytes 786440 | tf_op jit(solution)/shard_map/ppermute | solution.py:22
  64.3 54.3 %collective-permute-start.11 = (bf16[1,128,1024]{2,1,0:T(8,128)(2,1)S(1)}, bf16[1,128,1024]{2,1,0:T(8,128)(2,1)S(1)}, u32[]{:S(2)}, u32[]{:S(2)}) collective-permute-start(bf16[1,128,1024]{2,1,0:T(8,128)(2,1)S(1)} %get-tuple-element.122), channel_id=1, source_target_pairs={{0,12},{1,13},{2,14},{3,15},{4,8},{5,9},{6,10},{7,11},{8,4},{9,5},... | collective-permute-start | bytes 786440 | tf_op jit(solution)/shard_map/ppermute | solution.py:22
  65.5 58.7 %collective-permute-start.12 = (bf16[1,128,1024]{2,1,0:T(8,128)(2,1)S(1)}, bf16[1,128,1024]{2,1,0:T(8,128)(2,1)S(1)}, u32[]{:S(2)}, u32[]{:S(2)}) collective-permute-start(bf16[1,128,1024]{2,1,0:T(8,128)(2,1)S(1)} %get-tuple-element.121), channel_id=1, source_target_pairs={{0,13},{1,12},{2,15},{3,14},{4,9},{5,8},{6,11},{7,10},{8,5},{9,4},... | collective-permute-start | bytes 786440 | tf_op jit(solution)/shard_map/ppermute | solution.py:22
  90.5 39.3 %collective-permute-start.13 = (bf16[1,128,1024]{2,1,0:T(8,128)(2,1)S(1)}, bf16[1,128,1024]{2,1,0:T(8,128)(2,1)S(1)}, u32[]{:S(2)}, u32[]{:S(2)}) collective-permute-start(bf16[1,128,1024]{2,1,0:T(8,128)(2,1)S(1)} %get-tuple-element.120), channel_id=1, source_target_pairs={{0,14},{1,15},{2,12},{3,13},{4,10},{5,11},{6,8},{7,9},{8,6},{9,7},... | collective-permute-start | bytes 786440 | tf_op jit(solution)/shard_map/ppermute | solution.py:22
  101.7 33.3 %collective-permute-start.14 = (bf16[1,128,1024]{2,1,0:T(8,128)(2,1)S(1)}, bf16[1,128,1024]{2,1,0:T(8,128)(2,1)S(1)}, u32[]{:S(2)}, u32[]{:S(2)}) collective-permute-start(bf16[1,128,1024]{2,1,0:T(8,128)(2,1)S(1)} %get-tuple-element.119), channel_id=1, source_target_pairs={{0,15},{1,14},{2,13},{3,12},{4,11},{5,10},{6,9},{7,8},{8,7},{9,6},... | collective-permute-start | bytes 786440 | tf_op jit(solution)/shard_map/ppermute | solution.py:22
  141.6 3.1 copy-start.9
  158.5 9.8 %copy-start.8 = (s32[16,3]{0,1:T(4,128)S(1)}, s32[16,3]{0,1:T(4,128)}, u32[]{:S(2)}) copy-start(s32[16,3]{0,1:T(4,128)} %param.22) | copy-start | bytes 580
  158.5 10.0 %copy-start.10 = (f32[8]{0:T(128)S(1)}, f32[8]{0:T(128)}, u32[]{:S(2)}) copy-start(f32[8]{0:T(128)} %param.21) | copy-start | bytes 100
  158.5 95.2 %collective-permute-start.15 = (bf16[2,16,128,512]{2,3,1,0:T(8,128)(2,1)}, bf16[2,16,128,512]{2,3,1,0:T(8,128)(2,1)}, u32[]{:S(2)}, u32[]{:S(2)}) collective-permute-start(bf16[2,16,128,512]{2,3,1,0:T(8,128)(2,1)} %pad_maximum_fusion.2), channel_id=1, source_target_pairs={{0,1},{1,2},{2,3},{3,4},{4,5},{5,6},{6,7},{7,8},{8,9},{9,10},{10,1... | collective-permute-start | bytes 12582920 | tf_op jit(solution)/shard_map/ppermute | solution.py:34
  160.5 93.2 %collective-permute-start.16 = (bf16[2,16,128,512]{2,3,1,0:T(8,128)(2,1)}, bf16[2,16,128,512]{2,3,1,0:T(8,128)(2,1)}, u32[]{:S(2)}, u32[]{:S(2)}) collective-permute-start(bf16[2,16,128,512]{2,3,1,0:T(8,128)(2,1)} %pad_maximum_fusion.2), channel_id=1, source_target_pairs={{1,0},{2,1},{3,2},{4,3},{5,4},{6,5},{7,6},{8,7},{9,8},{10,9},{11,1... | collective-permute-start | bytes 12582920 | tf_op jit(solution)/shard_map/ppermute | solution.py:35
  260.0 5.8 %copy-start.3 = (bf16[4,4,128,8,64]{2,4,3,1,0:T(8,128)(2,1)S(1)}, bf16[4,4,128,8,64]{2,4,3,1,0:T(8,128)(2,1)}, u32[]{:S(2)}) copy-start(bf16[4,4,128,8,64]{2,4,3,1,0:T(8,128)(2,1)} %copy.22) | copy-start | bytes 6291460
  268.5 5.9 %copy-start.2 = (f32[4,8,128,384]{3,2,1,0:T(8,128)}, f32[4,8,128,384]{3,2,1,0:T(8,128)S(1)}, u32[]{:S(2)}) copy-start(f32[4,8,128,384]{3,2,1,0:T(8,128)S(1)} %get-tuple-element.192) | copy-start | bytes 18874372 | tf_op jit(solution)/shard_map/while
  268.5 3.1 copy-start.5
  286.7 6.0 %copy-start.2 = (f32[4,8,128,384]{3,2,1,0:T(8,128)}, f32[4,8,128,384]{3,2,1,0:T(8,128)S(1)}, u32[]{:S(2)}) copy-start(f32[4,8,128,384]{3,2,1,0:T(8,128)S(1)} %get-tuple-element.192) | copy-start | bytes 18874372 | tf_op jit(solution)/shard_map/while
  286.7 3.1 copy-start.5
  305.0 6.0 %copy-start.2 = (f32[4,8,128,384]{3,2,1,0:T(8,128)}, f32[4,8,128,384]{3,2,1,0:T(8,128)S(1)}, u32[]{:S(2)}) copy-start(f32[4,8,128,384]{3,2,1,0:T(8,128)S(1)} %get-tuple-element.192) | copy-start | bytes 18874372 | tf_op jit(solution)/shard_map/while
  305.0 3.1 copy-start.5
  323.3 6.0 %copy-start.2 = (f32[4,8,128,384]{3,2,1,0:T(8,128)}, f32[4,8,128,384]{3,2,1,0:T(8,128)S(1)}, u32[]{:S(2)}) copy-start(f32[4,8,128,384]{3,2,1,0:T(8,128)S(1)} %get-tuple-element.192) | copy-start | bytes 18874372 | tf_op jit(solution)/shard_map/while
  323.4 3.1 copy-start.5
  338.9 99.1 %slice-start = ((s8[6291456]{0:T(1024)(128)(4,1)}), s8[4194304]{0:T(1024)(128)(4,1)S(1)}, s32[]{:S(2)}) async-start(s8[6291456]{0:T(1024)(128)(4,1)} %bitcast.119), calls=%async_computation | async-start | bytes 8388608
  338.9 99.1 %slice-start.2 = ((s8[6291456]{0:T(1024)(128)(4,1)}), s8[4194304]{0:T(1024)(128)(4,1)S(1)}, s32[]{:S(2)}) async-start(s8[6291456]{0:T(1024)(128)(4,1)} %bitcast.123), calls=%async_computation.2 | async-start | bytes 8388608
  338.9 99.1 %slice-start.1 = ((s8[6291456]{0:T(1024)(128)(4,1)}), s8[2097152]{0:T(1024)(128)(4,1)S(1)}, s32[]{:S(2)}) async-start(s8[6291456]{0:T(1024)(128)(4,1)} %bitcast.119), calls=%async_computation.1 | async-start | bytes 4194304
  338.9 99.1 %slice-start.3 = ((s8[6291456]{0:T(1024)(128)(4,1)}), s8[2097152]{0:T(1024)(128)(4,1)S(1)}, s32[]{:S(2)}) async-start(s8[6291456]{0:T(1024)(128)(4,1)} %bitcast.123), calls=%async_computation.3 | async-start | bytes 4194304
  342.9 95.0 %collective-permute-start.17 = (bf16[2,16,128,512]{2,3,1,0:T(8,128)(2,1)S(1)}, bf16[2,16,128,512]{2,3,1,0:T(8,128)(2,1)S(1)}, u32[]{:S(2)}, u32[]{:S(2)}) collective-permute-start(bf16[2,16,128,512]{2,3,1,0:T(8,128)(2,1)S(1)} %get-tuple-element.113), channel_id=1, source_target_pairs={{0,1},{1,2},{2,3},{3,4},{4,5},{5,6},{6,7},{7,8},{8,9},{9,10},{10,1... | collective-permute-start | bytes 12582920 | tf_op jit(solution)/shard_map/ppermute | solution.py:43
  345.3 92.7 %collective-permute-start.18 = (bf16[2,16,128,512]{2,3,1,0:T(8,128)(2,1)S(1)}, bf16[2,16,128,512]{2,3,1,0:T(8,128)(2,1)S(1)}, u32[]{:S(2)}, u32[]{:S(2)}) collective-permute-start(bf16[2,16,128,512]{2,3,1,0:T(8,128)(2,1)S(1)} %get-tuple-element.114), channel_id=1, source_target_pairs={{1,0},{2,1},{3,2},{4,3},{5,4},{6,5},{7,6},{8,7},{9,8},{10,9},{11,1... | collective-permute-start | bytes 12582920 | tf_op jit(solution)/shard_map/ppermute | solution.py:43
  441.6 6.6 %copy-start.1 = (bf16[1024,512]{1,0:T(8,128)(2,1)S(1)}, bf16[1024,512]{1,0:T(8,128)(2,1)}, u32[]{:S(2)}) copy-start(bf16[1024,512]{1,0:T(8,128)(2,1)} %param.19) | copy-start | bytes 3145732
